TPU v7x, 256 devices: a whole 4x4x8 slice. The times are simulated.
256 devices in a mesh: enc: 16 (over z_hi, x), dec: 8 (over y, core), grp: 2 (over z_lo).
Axes of the slice: x: 4, y: 4, z: 8 (z_hi: 4, z_lo: 2; z = z_hi * 2 + z_lo), core: 2. Of those that a mesh axis runs over, the one named last changes fastest.
Arguments:
- images: bfloat16 [256, 4, 32, 1280], P(('enc', 'dec', 'grp')), may hold values from -6 to 6
- ln_gain: float32 [1280], replicated, may hold values from 0.1 to 1.9
- ln_bias: float32 [1280], replicated, may hold values from -3 to 3
- fc1_weight: bfloat16 [5120, 1280], P('enc'), may hold values from -0.15625 to 0.15625
- fc1_bias: float32 [5120], P('enc'), may hold values from -3 to 3
- fc2_weight: bfloat16 [5120, 1280], P('enc'), may hold values from -0.078125 to 0.078125
- fc2_bias: float32 [1280], replicated, may hold values from -3 to 3
- key_weight: bfloat16 [1280, 512], replicated, may hold values from -0.15625 to 0.15625
- value_weight: bfloat16 [1280, 512], replicated, may hold values from -0.15625 to 0.15625
- text: bfloat16 [64, 128, 8192], P(('enc', 'grp')), may hold values from -6 to 6
- query_weight: bfloat16 [8192, 4096], P('enc', 'dec'), may hold values from -0.0625 to 0.0625
- tiles: int32 [16, 8, 2], replicated, may hold values from 1 to 4, as said below
- links: int32 [64, 8], P(('enc', 'grp')), may hold values from 0 to 1, as said below
- lengths: int32 [64], P(('enc', 'grp')), may hold values from 1 to 128
- state_grads: bfloat16 [256, 4, 32, 1280], P(('enc', 'dec', 'grp')), may hold values from -0.125 to 0.125
Outputs:
- context: bfloat16 [64, 128, 4096], P(('enc', 'grp'), None, 'dec')
- fc1_grad: float32 [5120, 1280], P(('enc', 'dec', 'grp'))
- fc2_grad: float32 [5120, 1280], P(('enc', 'dec', 'grp'))
Inputs may be any that keep to these rules, and one draw needn't show every extreme that they name: The 16 images that share their last two indices have 40 tiles together, and one of them has 4. `links`: every text is linked to at least one image.
All inputs are finite; a program needn't handle non-finite values.
Results may differ from a plain program's by a relative error of at most 0.017.
Values may be sent and summed in bfloat16 or wider, within the bound.
No kernel may reach another device: no remote copies, remote signals or barrier semaphores. Data moves between devices by JAX's collectives and lax.ppermute only.
A program may use at most 128 MiB of HBM per device.

v0:
```python
import jax
import jax.numpy as jnp
import numpy as np
from jax import lax
from jax.sharding import PartitionSpec as P

HEADS = 32
KV_HEADS = 4
HD = 128
EPSILON = 1e-06


def laid_out(blocks, dim):
    blocks = jnp.moveaxis(blocks, 0, dim)
    dims = blocks.shape
    return blocks.reshape(*dims[:dim], dims[dim] * dims[dim + 1], *dims[dim + 2 :])


def one_gather(arrays, axis, dims):
    line = jnp.concatenate([a.reshape(-1) for a in arrays])
    lines, at, gathered = (lax.all_gather(line, axis), 0, [])
    for a, dim in zip(arrays, dims):
        blocks = lines[:, at : at + a.size].reshape(-1, *a.shape)
        gathered.append(laid_out(blocks, dim))
        at += a.size
    return tuple(gathered)


def in_blocks(array, dim, size):
    before, after = (array.shape[:dim], array.shape[dim + 1 :])
    return jnp.moveaxis(array.reshape(*before, size, -1, *after), dim, 0)


def summed_on_arrival(array, axis, dim):
    blocks = in_blocks(array, dim, lax.axis_size(axis))
    arrived = lax.all_to_all(blocks, axis, split_axis=0, concat_axis=0, tiled=True)
    return arrived.astype(jnp.float32).sum(axis=0)


def in_one_piece(arrays, axis, dim, along):
    both = jnp.concatenate(arrays, axis=along)
    whole, at, gathered = (summed_on_arrival(both, axis, dim), 0, [])
    for a in arrays:
        gathered.append(lax.slice_in_dim(whole, at, at + a.shape[along], axis=along))
        at += a.shape[along]
    return tuple(gathered)


def normalize_layer(values, gain, shift):
    middle = jnp.mean(values, axis=-1, keepdims=True)
    centered = values - middle
    spread = jnp.mean(centered * centered, axis=-1, keepdims=True)
    return centered * lax.rsqrt(spread + EPSILON) * gain + shift


def normalize_heads(values):
    return values * lax.rsqrt(jnp.mean(values * values, axis=-1, keepdims=True) + EPSILON)


def gelu_slope(values):
    return (
        0.5 * (1.0 + lax.erf(values * 0.7071067811865476))
        + values * jnp.exp(-0.5 * values * values) * 0.3989422804014327
    )


def encoder_rows(rows, fc1_weight, fc1_bias, fc2_weight):
    pre = (
        lax.dot_general(
            rows, fc1_weight, (((1,), (1,)), ((), ())), preferred_element_type=jnp.float32
        )
        + fc1_bias
    )
    hidden = jax.nn.gelu(pre, approximate=False).astype(jnp.bfloat16)
    partial_sum = jnp.dot(hidden, fc2_weight, preferred_element_type=jnp.float32)
    return (pre, hidden, partial_sum)


def weight_terms(rows, pre, hidden, cotangent, fc2_weight):
    hidden_grad = lax.dot_general(
        cotangent, fc2_weight, (((1,), (1,)), ((), ())), preferred_element_type=jnp.float32
    )
    second_term = lax.dot_general(
        hidden, cotangent, (((0,), (0,)), ((), ())), preferred_element_type=jnp.float32
    )
    pre_grad = (hidden_grad * gelu_slope(pre)).astype(jnp.bfloat16)
    first_term = lax.dot_general(
        pre_grad, rows, (((0,), (0,)), ((), ())), preferred_element_type=jnp.float32
    )
    return (first_term, second_term)


def project_heads(states, key_columns, value_columns, heads):
    width = states.shape[-1]
    key_raw = jnp.einsum(
        "rd,dhe->hre",
        states,
        key_columns.reshape(width, heads, HD),
        preferred_element_type=jnp.float32,
    )
    keys = normalize_heads(key_raw).astype(jnp.bfloat16)
    values = jnp.einsum(
        "rd,dhe->hre",
        states,
        value_columns.reshape(width, heads, HD),
        preferred_element_type=jnp.float32,
    ).astype(jnp.bfloat16)
    return (keys, values)


def on_device(
    images,
    ln_gain,
    ln_bias,
    fc1_weight,
    fc1_bias,
    fc2_weight,
    fc2_bias,
    key_weight,
    value_weight,
    text,
    query_weight,
    tiles,
    links,
    lengths,
    state_grads,
):
    dec_count = lax.axis_size("dec")
    enc_place = lax.axis_index("enc")
    dec_place = lax.axis_index("dec")
    grp_place = lax.axis_index("grp")
    slots = images.shape[1]
    patch = images.shape[2]
    width = images.shape[3]
    img_rows = slots * patch
    own_rows = images.reshape(img_rows, width)
    normed = normalize_layer(own_rows.astype(jnp.float32), ln_gain, ln_bias).astype(jnp.bfloat16)
    samples = text.shape[0]
    length = text.shape[1]
    text_rows = text.reshape(samples * length, text.shape[2])
    gathered, query_full = one_gather((normed, query_weight), "enc", (0, 0))
    query_raw = jnp.dot(text_rows, query_full, preferred_element_type=jnp.float32)
    tile_index = jnp.arange(slots)
    pre, hidden, partial_full = encoder_rows(gathered, fc1_weight, fc1_bias, fc2_weight)
    summed = lax.psum_scatter(
        partial_full.astype(jnp.bfloat16), "enc", scatter_dimension=0, tiled=True
    ).astype(jnp.float32)
    states = (own_rows.astype(jnp.float32) + summed + fc2_bias).astype(jnp.bfloat16)
    local_heads = query_weight.shape[1] // HD
    per_group = HEADS // KV_HEADS
    kv_local = max(1, local_heads // per_group)
    key_all, value_all = project_heads(states, key_weight, value_weight, KV_HEADS)
    table = np.array(
        [[peer * local_heads // per_group] for peer in range(dec_count)], np.int32
    ).reshape(-1)
    key_send = jnp.take(key_all, table, axis=0).reshape(dec_count, kv_local, img_rows, HD)
    value_send = jnp.take(value_all, table, axis=0).reshape(dec_count, kv_local, img_rows, HD)
    keys, values = (
        lax.all_to_all(key_send, "dec", split_axis=0, concat_axis=0, tiled=True),
        lax.all_to_all(value_send, "dec", split_axis=0, concat_axis=0, tiled=True),
    )
    heads_each = local_heads // kv_local
    queries = normalize_heads(query_raw.reshape(samples, length, local_heads, HD)).astype(
        jnp.bfloat16
    )
    queries = queries.reshape(samples, length, kv_local, heads_each, HD)
    dec_tiles = tiles[enc_place, :, grp_place]
    live_keys = tile_index[None, :] < dec_tiles[:, None]
    live_keys = jnp.broadcast_to(live_keys[:, :, None], (dec_count, slots, patch)).reshape(
        dec_count, img_rows
    )
    allowed = (links[:, :, None] > 0) & live_keys[None, :, :]
    scores = jnp.einsum(
        "sqghd,jgkd->sghjkq", queries, keys, preferred_element_type=jnp.float32
    ) * HD ** (-0.5)
    weights = jnp.where(allowed[:, None, None, :, :, None], jnp.exp(scores), 0.0)
    totals = jnp.sum(weights, axis=(3, 4), keepdims=True)
    probs = (weights / totals).astype(jnp.bfloat16)
    mixed = jnp.einsum("sghjkq,jgkd->sqghd", probs, values, preferred_element_type=jnp.float32)
    valid = jnp.arange(length)[None, :] < lengths[:, None]
    context = (
        jnp.where(valid[:, :, None, None, None], mixed, 0.0)
        .reshape(samples, length, local_heads * HD)
        .astype(jnp.bfloat16)
    )
    own_tiles = tiles[enc_place, dec_place, grp_place]
    own_live = jnp.broadcast_to((tile_index < own_tiles)[:, None, None], (slots, patch, 1)).reshape(
        img_rows, 1
    )
    cotangent = jnp.where(
        own_live, state_grads.reshape(img_rows, width), jnp.zeros((), state_grads.dtype)
    )
    all_cotangent = lax.all_gather(cotangent, "enc", axis=0, tiled=True)
    first_term, second_term = weight_terms(gathered, pre, hidden, all_cotangent, fc2_weight)
    fc1_grad, fc2_grad = in_one_piece(
        (first_term.astype(jnp.bfloat16), second_term.astype(jnp.bfloat16)), ("dec", "grp"), 0, 1
    )
    return (context, fc1_grad, fc2_grad)


def solution(mesh):
    in_specs = (
        P(("enc", "dec", "grp"), None, None, None),
        P(),
        P(),
        P("enc", None),
        P("enc"),
        P("enc", None),
        P(),
        P(),
        P(),
        P(("enc", "grp"), None, None),
        P("enc", "dec"),
        P(),
        P(("enc", "grp"), None),
        P(("enc", "grp")),
        P(("enc", "dec", "grp"), None, None, None),
    )
    out_specs = (
        P(("enc", "grp"), None, "dec"),
        P(("enc", "dec", "grp"), None),
        P(("enc", "dec", "grp"), None),
    )
    return jax.shard_map(
        on_device, mesh=mesh, in_specs=in_specs, out_specs=out_specs, check_vma=False
    )
```

profile of v0, /device:TPU:1, one launch (start us, length us, event | category | flops | bytes accessed | tf_op | source)
XLA Modules:
  0.0 430.2 jit_solution(6207940955061156679)
XLA Ops:
  8.4 2.2 reshape.204
  11.9 2.1 copy.50
  24.2 165.6 %all-gather.6.cloned.1.call-done = bf16[6815744]{0:T(1024)(128)(2,1)} async-done(((bf16[425984]{0:T(1024)(128)(2,1)}), bf16[6815744]{0:T(1024)(128)(2,1)}) %all-gather.6.cloned.1.call-update) | async-done | bytes 13631504 | tf_op jit(solution)/shard_map/all_gather | solution.py:21
  189.8 17.3 %reshape.221 = bf16[16,425984]{1,0:T(8,128)(2,1)} reshape(bf16[6815744]{0:T(1024)(128)(2,1)} %all-gather.6.cloned.1.call-done) | data formatting | bytes 27262976 | tf_op jit(solution)/shard_map/all_gather | solution.py:21
  207.1 4.4 %slice.20 = bf16[16,163840]{1,0:T(8,128)(2,1)} slice(bf16[16,425984]{1,0:T(8,128)(2,1)} %reshape.221), slice={[0:16], [0:163840]} | slice | bytes 10485760 | tf_op jit(solution)/shard_map/slice | solution.py:23
  211.5 5.7 %reshape_reshape.6 = bf16[2048,1280]{1,0:T(8,128)(2,1)} reshape(bf16[16,163840]{1,0:T(8,128)(2,1)} %slice.20) | data formatting | bytes 10485760 | tf_op jit(solution)/shard_map/reshape;reshape | solution.py:16
  217.2 10.3 %fusion.4 = (bf16[2048,320]{0,1:T(8,128)(2,1)S(1)}, f32[2048,320]{0,1:T(8,128)}) fusion(f32[320]{0:T(512)S(1)} %copy-done.10, bf16[2048,1280]{1,0:T(8,128)(2,1)} %reshape_reshape.6, bf16[320,1280]{1,0:T(8,128)(2,1)S(1)} %copy-done.8), kind=kOutput, calls=%fused_computation.16 | convolution fusion | flops 1720975360 | bytes 9995520 | tf_op jit(solution)/shard_map/dot_general | solution.py:69
  228.6 4.7 %convolution_convert_fusion = bf16[2048,1280]{1,0:T(8,128)(2,1)} fusion(bf16[2048,320]{0,1:T(8,128)(2,1)S(1)} %get-tuple-element.15, bf16[320,1280]{1,0:T(8,128)(2,1)S(1)} %copy-done.9), kind=kOutput, calls=%fused_computation.2 | convolution fusion | flops 1680343040 | bytes 7372800 | tf_op jit(solution)/shard_map/dot_general | solution.py:75
  233.3 51.3 %all-gather.4.cloned.1.call-done = bf16[2048,1280]{1,0:T(8,128)(2,1)} async-done(((bf16[128,1280]{1,0:T(8,128)(2,1)}), bf16[2048,1280]{1,0:T(8,128)(2,1)}) %all-gather.4.cloned.1.call-update) | async-done | bytes 5242896 | tf_op jit(solution)/shard_map/all_gather | solution.py:193
  284.6 5.7 %convolution_convert_fusion.1 = bf16[320,1280]{1,0:T(8,128)(2,1)} fusion(bf16[2048,320]{0,1:T(8,128)(2,1)} %copy-done.14, bf16[2048,1280]{1,0:T(8,128)(2,1)} %all-gather.4.cloned.1.call-done), kind=kOutput, calls=%fused_computation.12 | convolution fusion | flops 1678131200 | bytes 7372800 | tf_op jit(solution)/shard_map/dot_general | solution.py:83
  290.3 9.4 %convolution_convert_fusion.2 = bf16[320,1280]{1,0:T(8,128)(2,1)} fusion(bf16[2048,1280]{1,0:T(8,128)(2,1)} %reshape_reshape.6, bf16[2048,1280]{1,0:T(8,128)(2,1)} %all-gather.4.cloned.1.call-done, bf16[320,1280]{1,0:T(8,128)(2,1)S(1)} %copy-done.9, f32[2048,320]{0,1:T(8,128)} %get-tuple-element.16), kind=kOutput, calls=%fused_computation.13 | convolution fusion | flops 3362406400 | bytes 14745600 | tf_op jit(solution)/shard_map/dot_general | solution.py:87
  302.7 5.7 %all-to-all-start.2 = ((bf16[16,20,2560]{2,1,0:T(8,128)(2,1)}), bf16[16,20,2560]{2,1,0:T(8,128)(2,1)S(1)}, u32[]{:S(2)}, u32[]{:S(2)}) async-start(bf16[16,20,2560]{2,1,0:T(8,128)(2,1)} %reshape.202), calls=%async_computation.3 | async-start | bytes 3932160 | tf_op jit(solution)/shard_map/all_to_all | solution.py:36
  309.7 7.2 %slice.21 = bf16[16,262144]{1,0:T(8,128)(2,1)} slice(bf16[16,425984]{1,0:T(8,128)(2,1)} %reshape.221), slice={[0:16], [163840:425984]} | slice | bytes 16777216 | tf_op jit(solution)/shard_map/slice | solution.py:23
  316.9 8.0 %reshape_reshape.7 = bf16[8192,512]{1,0:T(8,128)(2,1)} reshape(bf16[16,262144]{1,0:T(8,128)(2,1)} %slice.21) | data formatting | bytes 16777216 | tf_op jit(solution)/shard_map/reshape;reshape | solution.py:16
  324.9 8.1 %fusion.52 = (f32[256,512]{0,1:T(8,128)}, f32[256,512]{0,1:T(8,128)}) fusion(bf16[8192,512]{1,0:T(8,128)(2,1)} %reshape_reshape.7, bf16[256,8192]{1,0:T(8,128)(2,1)} %bitcast.139), kind=kOutput, calls=%fused_computation.84 | convolution fusion | flops 2147614720 | bytes 13631488 | tf_op jit(solution)/shard_map/dot_general | solution.py:142
  333.0 2.1 mul.114
  339.5 27.2 %all-to-all-done.2 = bf16[16,20,2560]{2,1,0:T(8,128)(2,1)S(1)} async-done(((bf16[16,20,2560]{2,1,0:T(8,128)(2,1)}), bf16[16,20,2560]{2,1,0:T(8,128)(2,1)S(1)}, u32[]{:S(2)}, u32[]{:S(2)}) %all-to-all-start.2) | async-done | bytes 1638432 | tf_op jit(solution)/shard_map/all_to_all | solution.py:36
  367.7 25.6 %reduce-scatter.2.cloned.1.call-done = bf16[128,1280]{1,0:T(8,128)(2,1)} async-done(((bf16[2048,1280]{1,0:T(8,128)(2,1)}), bf16[128,1280]{1,0:T(8,128)(2,1)}) %reduce-scatter.2.cloned.1.call-update) | async-done | bytes 327696 | tf_op jit(solution)/shard_map/reduce_scatter | solution.py:145
  396.5 5.9 %all-to-all-start.1 = ((bf16[8,1,128,128]{2,3,1,0:T(8,128)(2,1)}), bf16[8,1,128,128]{2,3,1,0:T(8,128)(2,1)S(1)}, u32[]{:S(2)}, u32[]{:S(2)}) async-start(bf16[8,1,128,128]{2,3,1,0:T(8,128)(2,1)} %bitcast.14), calls=%async_computation.2 | async-start | bytes 524288 | tf_op jit(solution)/shard_map/all_to_all | solution.py:159
  405.4 3.6 all-to-all-done.1
  408.9 4.4 %all-to-all-start = ((bf16[8,1,128,128]{3,2,1,0:T(8,128)(2,1)}), bf16[8,1,128,128]{3,2,1,0:T(8,128)(2,1)S(1)}, u32[]{:S(2)}, u32[]{:S(2)}) async-start(bf16[8,1,128,128]{3,2,1,0:T(8,128)(2,1)} %bitcast.4), calls=%async_computation.1 | async-start | bytes 524288 | tf_op jit(solution)/shard_map/all_to_all | solution.py:160
  413.3 2.6 fusion
  415.9 3.9 all-to-all-done
  419.8 3.0 fusion.27
  (84 shorter events, 30.4 us)
Async XLA Ops:
  7.2 387.4 %copy-start = (bf16[1280,512]{1,0:T(8,128)(2,1)S(1)}, bf16[1280,512]{1,0:T(8,128)(2,1)}, u32[]{:S(2)}) copy-start(bf16[1280,512]{1,0:T(8,128)(2,1)} %param.25) | copy-start | bytes 3932164
  7.2 6.8 %copy-start.4 = (f32[1280]{0:T(1024)S(1)}, f32[1280]{0:T(1024)}, u32[]{:S(2)}) copy-start(f32[1280]{0:T(1024)} %param.20) | copy-start | bytes 15364
  7.2 6.9 %copy-start.5 = (f32[1280]{0:T(1024)S(1)}, f32[1280]{0:T(1024)}, u32[]{:S(2)}) copy-start(f32[1280]{0:T(1024)} %param.19) | copy-start | bytes 15364
  7.2 182.6 %all-gather.6.cloned.1.call-start = ((), (), s32[]{:S(2)}) async-start(), calls=%async_computation.6 | async-start | bytes 14483456 | tf_op jit(solution)/shard_map/all_gather | solution.py:21
  19.3 1.5 copy-start.1
  19.3 2.6 copy-start.6
  20.8 2.5 copy-start.2
  21.8 262.8 %all-gather.4.cloned.1.call-start = ((), (), s32[]{:S(2)}) async-start(), calls=%async_computation.5 | async-start | bytes 5570560 | tf_op jit(solution)/shard_map/all_gather | solution.py:193
  24.2 369.2 %reduce-scatter.2.cloned.1.call-start = ((), (), s32[]{:S(2)}) async-start(), calls=%async_computation.4 | async-start | bytes 5570560 | tf_op jit(solution)/shard_map/reduce_scatter | solution.py:145
  211.4 5.7 %copy-start.8 = (bf16[320,1280]{1,0:T(8,128)(2,1)S(1)}, bf16[320,1280]{1,0:T(8,128)(2,1)}, u32[]{:S(2)}) copy-start(bf16[320,1280]{1,0:T(8,128)(2,1)} %param.21) | copy-start | bytes 2457604
  211.4 5.7 %copy-start.10 = (f32[320]{0:T(512)S(1)}, f32[320]{0:T(512)}, u32[]{:S(2)}) copy-start(f32[320]{0:T(512)} %param.22) | copy-start | bytes 3844
  217.1 11.4 %copy-start.9 = (bf16[320,1280]{1,0:T(8,128)(2,1)S(1)}, bf16[320,1280]{1,0:T(8,128)(2,1)}, u32[]{:S(2)}) copy-start(bf16[320,1280]{1,0:T(8,128)(2,1)} %param.23) | copy-start | bytes 2457604
  227.5 1.1 copy-start.14
  302.7 6.2 %copy-start.11 = (s32[2,8]{1,0:T(2,128)S(1)}, s32[2,8]{1,0:T(2,128)}, u32[]{:S(2)}) copy-start(s32[2,8]{1,0:T(2,128)} %param.30) | copy-start | bytes 196
  302.7 6.3 %copy-start.7 = (s32[8]{0:T(128)S(1)}, s32[8]{0:T(128)}, u32[]{:S(2)}) copy-start(s32[8]{0:T(128)} %constant.140) | copy-start | bytes 100
  302.7 6.3 %copy-start.12 = (s32[2]{0:T(128)S(1)}, s32[2]{0:T(128)}, u32[]{:S(2)}) copy-start(s32[2]{0:T(128)} %param.31) | copy-start | bytes 28
  302.7 64.0 %all-to-all-start.2 = ((bf16[16,20,2560]{2,1,0:T(8,128)(2,1)}), bf16[16,20,2560]{2,1,0:T(8,128)(2,1)S(1)}, u32[]{:S(2)}, u32[]{:S(2)}) async-start(bf16[16,20,2560]{2,1,0:T(8,128)(2,1)} %reshape.202), calls=%async_computation.3 | async-start | bytes 3932160 | tf_op jit(solution)/shard_map/all_to_all | solution.py:36
  336.5 56.9 %copy-start.3 = (f32[1280]{0:T(1024)S(1)}, f32[1280]{0:T(1024)}, u32[]{:S(2)}) copy-start(f32[1280]{0:T(1024)} %param.24) | copy-start | bytes 15364
  396.5 12.4 %all-to-all-start.1 = ((bf16[8,1,128,128]{2,3,1,0:T(8,128)(2,1)}), bf16[8,1,128,128]{2,3,1,0:T(8,128)(2,1)S(1)}, u32[]{:S(2)}, u32[]{:S(2)}) async-start(bf16[8,1,128,128]{2,3,1,0:T(8,128)(2,1)} %bitcast.14), calls=%async_computation.2 | async-start | bytes 524288 | tf_op jit(solution)/shard_map/all_to_all | solution.py:159
  408.9 10.9 %all-to-all-start = ((bf16[8,1,128,128]{3,2,1,0:T(8,128)(2,1)}), bf16[8,1,128,128]{3,2,1,0:T(8,128)(2,1)S(1)}, u32[]{:S(2)}, u32[]{:S(2)}) async-start(bf16[8,1,128,128]{3,2,1,0:T(8,128)(2,1)} %bitcast.4), calls=%async_computation.1 | async-start | bytes 524288 | tf_op jit(solution)/shard_map/all_to_all | solution.py:160
  413.3 6.5 %copy-start.13 = (pred[2,128]{1,0:T(4,128)(4,1)S(1)}, pred[2,128]{1,0:T(4,128)(4,1)}, u32[]{:S(2)}) copy-start(pred[2,128]{1,0:T(4,128)(4,1)} %iota_compare_fusion.1) | copy-start | bytes 772
Sparse Core Ops, SparseCore 0:
  22.0 167.8 all-gather.5
  192.3 92.2 all-gather.3
  288.3 105.0 reduce-scatter.1
where the time goes:
time: 431 us; the launch traced here: 430 us
  waiting for transfers between devices  277 us (64%)
  local copies, waits for them, and re-layouts  64.3 us (15%)
  matrix products  46.2 us (11%)
  starting transfers between devices  16 us (4%)
  between operations  14 us (3%)
  other arithmetic  12.4 us (3%)
    all_gather x1, waiting for transfers between devices, one_gather(): lines, at, gathered = (lax.all_gather(line, axis), 0, [])  166 us
    all_gather x1, waiting for transfers between devices, on_device(): all_cotangent = lax.all_gather(cotangent, 'enc', axis=0, tiled=True)  51.3 us
    all_to_all x1, waiting for transfers between devices, summed_on_arrival(): lax.all_to_all(blocks, axis, split_axis=0, concat_axis=0, tiled=True)  27.2 us
    reduce_scatter x1, waiting for transfers between devices, on_device(): lax.psum_scatter(partial_full.astype(jnp.bfloat16), 'enc', scatter_dimens...  25.6 us
    all_gather x1, local copies, waits for them, and re-layouts, one_gather(): lines, at, gathered = (lax.all_gather(line, axis), 0, [])  17.3 us
    another operation x2, local copies, waits for them, and re-layouts, laid_out(): blocks.reshape(*dims[:dim], dims[dim] * dims[dim + 1], *dims[dim + 2:])  13.7 us
    slice x2, local copies, waits for them, and re-layouts, one_gather(): blocks = lines[:, at:at + a.size].reshape(-1, *a.shape)  11.6 us
    dot_general x1, matrix products, encoder_rows(): lax.dot_general(rows, fc1_weight, (((1,), (1,)), ((), ())), preferred_ele...  10.3 us
  transfers between devices with their start and end apart: 6, of which 6 were waited for; matrix products, arithmetic and copies ran while one was open for 23% of the time, Pallas kernels for 0%

commit v1 on v0

--- a/solution.py
+++ b/solution.py
@@ -190,7 +190,9 @@
     cotangent = jnp.where(
         own_live, state_grads.reshape(img_rows, width), jnp.zeros((), state_grads.dtype)
     )
-    all_cotangent = lax.all_gather(cotangent, "enc", axis=0, tiled=True)
+    all_cotangent = jnp.concatenate(
+        lax.all_to_all(jnp.stack([cotangent] * lax.axis_size("enc")), "enc", 0, 0), axis=0
+    )
     first_term, second_term = weight_terms(gathered, pre, hidden, all_cotangent, fc2_weight)
     fc1_grad, fc2_grad = in_one_piece(
         (first_term.astype(jnp.bfloat16), second_term.astype(jnp.bfloat16)), ("dec", "grp"), 0, 1

time: 431 us -> 481 us (1.12)
  waiting for transfers between devices: 277 us -> 314 us
  starting transfers between devices: 16 us -> 27.2 us
    all_gather x1, waiting for transfers between devices: 166 us -> 256 us  [one_gather(): lines, at, gathered = (lax.all_gather(line, axis), 0, [])]
    all_gather x1 -> x0, waiting for transfers between devices: 51.3 us -> none  [on_device(): all_cotangent = lax.all_gather(cotangent, 'enc', axis=0, tiled=True)]
    all_to_all x0 -> x1, starting transfers between devices: none -> 11.6 us  [on_device(): lax.all_to_all(jnp.stack([cotangent] * lax.axis_size('enc')), 'enc', 0, 0)]
  transfers between devices with their start and end apart: 6 -> 6, of which waited for: 6 -> 5; matrix products, arithmetic and copies ran while one was open for 23% -> 21% of each run, Pallas kernels for 0% -> 0%
where the time goes in v1:
time: 481 us; the launch traced here: 480 us
  waiting for transfers between devices  314 us (65%)
  local copies, waits for them, and re-layouts  67.1 us (14%)
  matrix products  46.3 us (10%)
  starting transfers between devices  27.2 us (6%)
  between operations  14.3 us (3%)
  other arithmetic  11.8 us (2%)
    all_gather x1, waiting for transfers between devices, one_gather(): lines, at, gathered = (lax.all_gather(line, axis), 0, [])  256 us
    all_to_all x1, waiting for transfers between devices, summed_on_arrival(): lax.all_to_all(blocks, axis, split_axis=0, concat_axis=0, tiled=True)  25.9 us
    reduce_scatter x1, waiting for transfers between devices, on_device(): lax.psum_scatter(partial_full.astype(jnp.bfloat16), 'enc', scatter_dimens...  24.6 us
    all_gather x1, local copies, waits for them, and re-layouts, one_gather(): lines, at, gathered = (lax.all_gather(line, axis), 0, [])  17.2 us
    another operation x2, local copies, waits for them, and re-layouts, laid_out(): blocks.reshape(*dims[:dim], dims[dim] * dims[dim + 1], *dims[dim + 2:])  13.7 us
    all_to_all x1, starting transfers between devices, on_device(): lax.all_to_all(jnp.stack([cotangent] * lax.axis_size('enc')), 'enc', 0, 0)  11.6 us
    slice x2, local copies, waits for them, and re-layouts, one_gather(): blocks = lines[:, at:at + a.size].reshape(-1, *a.shape)  11.5 us
    dot_general x1, matrix products, encoder_rows(): lax.dot_general(rows, fc1_weight, (((1,), (1,)), ((), ())), preferred_ele...  10.3 us
  transfers between devices with their start and end apart: 6, of which 5 were waited for; matrix products, arithmetic and copies ran while one was open for 21% of the time, Pallas kernels for 0%

profile of v1, /device:TPU:1, one launch (start us, length us, event | category | flops | bytes accessed | tf_op | source)
XLA Modules:
  0.0 480.3 jit_solution(7580561958040609570)
XLA Ops:
  8.4 2.2 reshape.217
  23.4 2.9 stack.2
  26.3 11.6 %all-to-all-start.2 = ((bf16[16,128,1280]{2,1,0:T(8,128)(2,1)}), bf16[16,128,1280]{2,1,0:T(8,128)(2,1)}, u32[]{:S(2)}, u32[]{:S(2)}) async-start(bf16[16,128,1280]{2,1,0:T(8,128)(2,1)} %stack.2), calls=%async_computation.3 | async-start | bytes 10485760 | tf_op jit(solution)/shard_map/all_to_all | solution.py:194
  38.2 255.6 %all-gather.3.cloned.1.call-done = bf16[6815744]{0:T(1024)(128)(2,1)} async-done(((bf16[425984]{0:T(1024)(128)(2,1)}), bf16[6815744]{0:T(1024)(128)(2,1)}) %all-gather.3.cloned.1.call-update) | async-done | bytes 13631504 | tf_op jit(solution)/shard_map/all_gather | solution.py:21
  293.8 17.2 %reshape.234 = bf16[16,425984]{1,0:T(8,128)(2,1)} reshape(bf16[6815744]{0:T(1024)(128)(2,1)} %all-gather.3.cloned.1.call-done) | data formatting | bytes 27262976 | tf_op jit(solution)/shard_map/all_gather | solution.py:21
  311.0 4.2 slice.20
  315.2 5.7 %reshape_reshape.6 = bf16[2048,1280]{1,0:T(8,128)(2,1)} reshape(bf16[16,163840]{1,0:T(8,128)(2,1)} %slice.20) | data formatting | bytes 10485760 | tf_op jit(solution)/shard_map/reshape;reshape | solution.py:16
  320.9 10.3 %fusion.4 = (bf16[2048,320]{0,1:T(8,128)(2,1)S(1)}, f32[2048,320]{0,1:T(8,128)}) fusion(f32[320]{0:T(512)S(1)} %copy-done.10, bf16[2048,1280]{1,0:T(8,128)(2,1)} %reshape_reshape.6, bf16[320,1280]{1,0:T(8,128)(2,1)S(1)} %copy-done.8), kind=kOutput, calls=%fused_computation.16 | convolution fusion | flops 1720975360 | bytes 9995520 | tf_op jit(solution)/shard_map/dot_general | solution.py:69
  332.3 4.7 convolution_convert_fusion
  337.1 5.7 %convolution_convert_fusion.1 = bf16[320,1280]{1,0:T(8,128)(2,1)} fusion(bf16[2048,320]{0,1:T(8,128)(2,1)} %copy-done.14, bf16[2048,1280]{1,0:T(8,128)(2,1)} %bitcast.31), kind=kOutput, calls=%fused_computation.12 | convolution fusion | flops 1678131200 | bytes 7372800 | tf_op jit(solution)/shard_map/dot_general | solution.py:83
  342.8 9.4 %convolution_convert_fusion.2 = bf16[320,1280]{1,0:T(8,128)(2,1)} fusion(bf16[2048,1280]{1,0:T(8,128)(2,1)} %reshape_reshape.6, bf16[2048,1280]{1,0:T(8,128)(2,1)} %bitcast.31, bf16[320,1280]{1,0:T(8,128)(2,1)S(1)} %copy-done.9, f32[2048,320]{0,1:T(8,128)} %get-tuple-element.16), kind=kOutput, calls=%fused_computation.13 | convolution fusion | flops 3362406400 | bytes 14745600 | tf_op jit(solution)/shard_map/dot_general | solution.py:87
  355.2 5.2 %all-to-all-start.3 = ((bf16[16,20,2560]{2,1,0:T(8,128)(2,1)}), bf16[16,20,2560]{2,1,0:T(8,128)(2,1)S(1)}, u32[]{:S(2)}, u32[]{:S(2)}) async-start(bf16[16,20,2560]{2,1,0:T(8,128)(2,1)} %reshape.215), calls=%async_computation.4 | async-start | bytes 3932160 | tf_op jit(solution)/shard_map/all_to_all | solution.py:36
  361.8 7.2 %slice.21 = bf16[16,262144]{1,0:T(8,128)(2,1)} slice(bf16[16,425984]{1,0:T(8,128)(2,1)} %reshape.234), slice={[0:16], [163840:425984]} | slice | bytes 16777216 | tf_op jit(solution)/shard_map/slice | solution.py:23
  369.1 8.0 %reshape_reshape.7 = bf16[8192,512]{1,0:T(8,128)(2,1)} reshape(bf16[16,262144]{1,0:T(8,128)(2,1)} %slice.21) | data formatting | bytes 16777216 | tf_op jit(solution)/shard_map/reshape;reshape | solution.py:16
  377.0 8.2 %fusion.52 = (f32[256,512]{0,1:T(8,128)}, f32[256,512]{0,1:T(8,128)}) fusion(bf16[8192,512]{1,0:T(8,128)(2,1)} %reshape_reshape.7, bf16[256,8192]{1,0:T(8,128)(2,1)} %bitcast.140), kind=kOutput, calls=%fused_computation.84 | convolution fusion | flops 2147614720 | bytes 13631488 | tf_op jit(solution)/shard_map/dot_general | solution.py:142
  385.2 2.1 mul.114
  391.8 25.9 %all-to-all-done.3 = bf16[16,20,2560]{2,1,0:T(8,128)(2,1)S(1)} async-done(((bf16[16,20,2560]{2,1,0:T(8,128)(2,1)}), bf16[16,20,2560]{2,1,0:T(8,128)(2,1)S(1)}, u32[]{:S(2)}, u32[]{:S(2)}) %all-to-all-start.3) | async-done | bytes 1638432 | tf_op jit(solution)/shard_map/all_to_all | solution.py:36
  418.7 24.6 %reduce-scatter.2.cloned.1.call-done = bf16[128,1280]{1,0:T(8,128)(2,1)} async-done(((bf16[2048,1280]{1,0:T(8,128)(2,1)}), bf16[128,1280]{1,0:T(8,128)(2,1)}) %reduce-scatter.2.cloned.1.call-update) | async-done | bytes 327696 | tf_op jit(solution)/shard_map/reduce_scatter | solution.py:145
  446.4 5.8 %all-to-all-start.1 = ((bf16[8,1,128,128]{2,3,1,0:T(8,128)(2,1)}), bf16[8,1,128,128]{2,3,1,0:T(8,128)(2,1)S(1)}, u32[]{:S(2)}, u32[]{:S(2)}) async-start(bf16[8,1,128,128]{2,3,1,0:T(8,128)(2,1)} %bitcast.14), calls=%async_computation.2 | async-start | bytes 524288 | tf_op jit(solution)/shard_map/all_to_all | solution.py:159
  455.1 3.6 all-to-all-done.1
  458.7 4.4 all-to-all-start
  463.1 2.6 fusion
  465.7 3.9 all-to-all-done
  469.6 3.0 fusion.27
  (84 shorter events, 31.9 us)
Async XLA Ops:
  7.2 437.3 %copy-start = (bf16[1280,512]{1,0:T(8,128)(2,1)S(1)}, bf16[1280,512]{1,0:T(8,128)(2,1)}, u32[]{:S(2)}) copy-start(bf16[1280,512]{1,0:T(8,128)(2,1)} %param.25) | copy-start | bytes 3932164
  7.2 6.8 %copy-start.4 = (f32[1280]{0:T(1024)S(1)}, f32[1280]{0:T(1024)}, u32[]{:S(2)}) copy-start(f32[1280]{0:T(1024)} %param.20) | copy-start | bytes 15364
  7.2 6.9 %copy-start.5 = (f32[1280]{0:T(1024)S(1)}, f32[1280]{0:T(1024)}, u32[]{:S(2)}) copy-start(f32[1280]{0:T(1024)} %param.19) | copy-start | bytes 15364
  7.2 286.6 %all-gather.3.cloned.1.call-start = ((), (), s32[]{:S(2)}) async-start(), calls=%async_computation.6 | async-start | bytes 14483456 | tf_op jit(solution)/shard_map/all_gather | solution.py:21
  19.4 1.5 copy-start.1
  19.4 2.5 copy-start.6
  20.9 2.5 copy-start.2
  26.3 310.7 %all-to-all-start.2 = ((bf16[16,128,1280]{2,1,0:T(8,128)(2,1)}), bf16[16,128,1280]{2,1,0:T(8,128)(2,1)}, u32[]{:S(2)}, u32[]{:S(2)}) async-start(bf16[16,128,1280]{2,1,0:T(8,128)(2,1)} %stack.2), calls=%async_computation.3 | async-start | bytes 10485760 | tf_op jit(solution)/shard_map/all_to_all | solution.py:194
  38.0 405.3 %reduce-scatter.2.cloned.1.call-start = ((), (), s32[]{:S(2)}) async-start(), calls=%async_computation.5 | async-start | bytes 5570560 | tf_op jit(solution)/shard_map/reduce_scatter | solution.py:145
  315.2 5.7 %copy-start.8 = (bf16[320,1280]{1,0:T(8,128)(2,1)S(1)}, bf16[320,1280]{1,0:T(8,128)(2,1)}, u32[]{:S(2)}) copy-start(bf16[320,1280]{1,0:T(8,128)(2,1)} %param.21) | copy-start | bytes 2457604
  315.2 5.7 %copy-start.10 = (f32[320]{0:T(512)S(1)}, f32[320]{0:T(512)}, u32[]{:S(2)}) copy-start(f32[320]{0:T(512)} %param.22) | copy-start | bytes 3844
  320.9 11.4 %copy-start.9 = (bf16[320,1280]{1,0:T(8,128)(2,1)S(1)}, bf16[320,1280]{1,0:T(8,128)(2,1)}, u32[]{:S(2)}) copy-start(bf16[320,1280]{1,0:T(8,128)(2,1)} %param.23) | copy-start | bytes 2457604
  331.2 1.1 copy-start.14
  355.2 5.8 %copy-start.11 = (s32[2,8]{1,0:T(2,128)S(1)}, s32[2,8]{1,0:T(2,128)}, u32[]{:S(2)}) copy-start(s32[2,8]{1,0:T(2,128)} %param.30) | copy-start | bytes 196
  355.2 5.9 %copy-start.7 = (s32[8]{0:T(128)S(1)}, s32[8]{0:T(128)}, u32[]{:S(2)}) copy-start(s32[8]{0:T(128)} %constant.140) | copy-start | bytes 100
  355.2 5.9 %copy-start.12 = (s32[2]{0:T(128)S(1)}, s32[2]{0:T(128)}, u32[]{:S(2)}) copy-start(s32[2]{0:T(128)} %param.31) | copy-start | bytes 28
  355.2 62.5 %all-to-all-start.3 = ((bf16[16,20,2560]{2,1,0:T(8,128)(2,1)}), bf16[16,20,2560]{2,1,0:T(8,128)(2,1)S(1)}, u32[]{:S(2)}, u32[]{:S(2)}) async-start(bf16[16,20,2560]{2,1,0:T(8,128)(2,1)} %reshape.215), calls=%async_computation.4 | async-start | bytes 3932160 | tf_op jit(solution)/shard_map/all_to_all | solution.py:36
  388.7 54.6 %copy-start.3 = (f32[1280]{0:T(1024)S(1)}, f32[1280]{0:T(1024)}, u32[]{:S(2)}) copy-start(f32[1280]{0:T(1024)} %param.24) | copy-start | bytes 15364
  446.4 12.3 %all-to-all-start.1 = ((bf16[8,1,128,128]{2,3,1,0:T(8,128)(2,1)}), bf16[8,1,128,128]{2,3,1,0:T(8,128)(2,1)S(1)}, u32[]{:S(2)}, u32[]{:S(2)}) async-start(bf16[8,1,128,128]{2,3,1,0:T(8,128)(2,1)} %bitcast.14), calls=%async_computation.2 | async-start | bytes 524288 | tf_op jit(solution)/shard_map/all_to_all | solution.py:159
  458.7 10.9 %all-to-all-start = ((bf16[8,1,128,128]{3,2,1,0:T(8,128)(2,1)}), bf16[8,1,128,128]{3,2,1,0:T(8,128)(2,1)S(1)}, u32[]{:S(2)}, u32[]{:S(2)}) async-start(bf16[8,1,128,128]{3,2,1,0:T(8,128)(2,1)} %bitcast.4), calls=%async_computation.1 | async-start | bytes 524288 | tf_op jit(solution)/shard_map/all_to_all | solution.py:160
  463.1 6.5 %copy-start.13 = (pred[2,128]{1,0:T(4,128)(4,1)S(1)}, pred[2,128]{1,0:T(4,128)(4,1)}, u32[]{:S(2)}) copy-start(pred[2,128]{1,0:T(4,128)(4,1)} %iota_compare_fusion.1) | copy-start | bytes 772
Sparse Core Ops, SparseCore 0:
  22.0 271.7 all-gather.2
  337.2 106.0 reduce-scatter.1
